TPU v7x, 32 devices: a whole 2x2x4 slice. The times are simulated.
32 devices in a mesh: rows: 16 (over z, y, core), cols: 2 (over x).
Axes of the slice: x: 2, y: 2, z: 4, core: 2. Of those that a mesh axis runs over, the one named last changes fastest.
Arguments:
- features: bfloat16 [4096, 128], P('rows', 'cols'), may hold values from -6 to 6
- adj_tiles: bfloat16 [1536, 128, 128], P('rows'), may hold values from -0.109375 to 0.109375
- tile_src: int32 [1536], P('rows'), may hold values from 0 to 31, as said below
- tile_dst: int32 [1536], P('rows'), may hold values from 0 to 1, as said below
- tile_count: int32 [16], P('rows'), may hold values from 24 to 96, as said below
- cluster_size: int32 [32], P('rows'), may hold values from 64 to 128, as said below
- weight: bfloat16 [128, 256], P(None, 'cols'), may hold values from -0.5 to 0.5
- bias: float32 [256], P('cols'), may hold values from -3 to 3
- grad_out: bfloat16 [4096, 256], P('rows', 'cols'), may hold values from -6 to 6
Outputs:
- hidden: bfloat16 [4096, 256], P('rows', 'cols')
- grad_weight: float32 [128, 256], P(None, 'cols')
- grad_bias: float32 [256], P('cols')
- grad_features: bfloat16 [4096, 128], P('rows', 'cols')
Inputs may be any that keep to these rules, and one draw needn't show every extreme that they name: In row group r, slots 0 to tile_count[r] - 1 of its 96 slots hold tiles, in non-decreasing order of tile_src; the later slots are unused: their tile_src and tile_dst hold 0, and their adj_tiles hold arbitrary values that must not contribute. A used slot's column cluster belongs to row group r itself or to a row group whose index differs from r in exactly one bit (row group g holds clusters g * 2 to g * 2 + 1). Equal (row, column) pairs may repeat and then add. `tile_dst`: unused slots hold 0. `tile_count`: some row groups use all 96 slots. `cluster_size`: the real nodes of a cluster are its first ones; some cluster is full.
All inputs are finite; a program needn't handle non-finite values.
Results may differ from a plain program's by a relative error of at most 0.006.
Values may be sent and summed in bfloat16 or wider, within the bound.
No kernel may reach another device: no remote copies, remote signals or barrier semaphores. Data moves between devices by JAX's collectives and lax.ppermute only.
A program may use at most 64 MiB of HBM per device.

v0:
```python
import math
import jax
import jax.numpy as jnp
from jax import lax
from jax.sharding import PartitionSpec as P

TILE_GROUP = 16


def partner(shard, axis, distance):
    return lax.ppermute(shard, axis, [(i, i ^ 1 << distance) for i in range(lax.axis_size(axis))])


def sweep_slots(first_slot, last_slot, work, totals):
    turn_count = (last_slot - first_slot + TILE_GROUP - 1) // TILE_GROUP

    def one_turn(turn_index, carried):
        slot_ids = first_slot + turn_index * TILE_GROUP + jnp.arange(TILE_GROUP, dtype=jnp.int32)
        return work(carried, slot_ids, slot_ids < last_slot)

    return lax.fori_loop(0, jnp.maximum(turn_count, 0), one_turn, totals)


def slot_bounds(sources, first_slot, last_slot, low_cluster, high_cluster):
    positions = jnp.arange(sources.shape[0], dtype=jnp.int32)
    inside = (positions >= first_slot) & (positions < last_slot)
    below_low = jnp.sum((inside & (sources < low_cluster)).astype(jnp.int32))
    below_high = jnp.sum((inside & (sources < high_cluster)).astype(jnp.int32))
    return (first_slot + below_low, first_slot + below_high)


def neighbour_slots(sources, own_group, per_group, levels):
    group_of = sources // per_group
    within = sources - group_of * per_group
    differs = jnp.bitwise_xor(group_of, own_group)
    level = jnp.zeros_like(sources)
    for bit in range(levels):
        level = level + (bit + 1) * (differs == 1 << bit).astype(jnp.int32)
    return level * per_group + within


def gather_products(
    totals, tile_data, sources, targets, slot_ids, is_valid, row_table, base_cluster
):
    clamped = jnp.minimum(slot_ids, tile_data.shape[0] - 1)
    tile_block = tile_data[clamped]
    from_rows = jnp.clip(sources[clamped] - base_cluster, 0, row_table.shape[0] - 1)
    products = jnp.einsum(
        "tij,tjf->tif", tile_block, row_table[from_rows], preferred_element_type=jnp.float32
    )
    placed = jnp.where(is_valid, targets[clamped], totals.shape[0])
    return totals.at[placed].add(products, mode="drop")


def spread_products(
    totals, tile_data, sources, targets, slot_ids, is_valid, grad_table, base_cluster
):
    clamped = jnp.minimum(slot_ids, tile_data.shape[0] - 1)
    tile_block = tile_data[clamped]
    products = jnp.einsum(
        "tji,tjf->tif", tile_block, grad_table[targets[clamped]], preferred_element_type=jnp.float32
    )
    placed = jnp.where(is_valid, sources[clamped] - base_cluster, totals.shape[0])
    return totals.at[placed].add(products, mode="drop")


def local(
    features, adj_tiles, tile_src, tile_dst, tile_count, cluster_size, weight, bias, grad_out
):
    clusters_here = cluster_size.shape[0]
    tile_width = adj_tiles.shape[1]
    feat_half = features.shape[1]
    node_rows = clusters_here * tile_width
    node_ids = jnp.arange(tile_width, dtype=jnp.int32)
    live_node = (node_ids[None, :] < cluster_size[:, None]).astype(jnp.float32)[:, :, None]
    live_flat = live_node.reshape(node_rows, 1)
    masked = (
        features.reshape(clusters_here, tile_width, feat_half).astype(jnp.float32) * live_node
    ).astype(jnp.bfloat16)
    my_count = tile_count[0]
    levels = lax.axis_size("rows").bit_length() - 1
    local_slots = neighbour_slots(tile_src, lax.axis_index("rows"), clusters_here, levels)
    zero_totals = jnp.zeros((clusters_here, tile_width, feat_half), jnp.float32)
    whole_rows = lax.all_gather(masked, "rows", axis=0, tiled=True)
    row_count = whole_rows.shape[0]
    first_slot, last_slot = slot_bounds(tile_src, 0, my_count, 0, 0 + row_count)
    own_totals = sweep_slots(
        first_slot,
        last_slot,
        lambda totals, slot_ids, is_valid: gather_products(
            totals, adj_tiles, tile_src, tile_dst, slot_ids, is_valid, whole_rows, 0
        ),
        zero_totals,
    )
    agg_local = own_totals.reshape(node_rows, feat_half).astype(jnp.bfloat16)
    agg_full = lax.all_gather(agg_local, "cols", axis=1, tiled=True)
    pre_activation = jnp.dot(agg_full, weight, preferred_element_type=jnp.float32) + bias
    sigmoid_pre = jax.nn.sigmoid(pre_activation)
    hidden = (pre_activation * sigmoid_pre * live_flat).astype(jnp.bfloat16)
    grad_pre = (
        grad_out.astype(jnp.float32)
        * sigmoid_pre
        * (1.0 + pre_activation * (1.0 - sigmoid_pre))
        * live_flat
    ).astype(jnp.bfloat16)
    weight_term = lax.dot_general(
        agg_full, grad_pre, (((0,), (0,)), ((), ())), preferred_element_type=jnp.float32
    )
    bias_term = jnp.sum(grad_pre.astype(jnp.float32), axis=0)
    weight_total, bias_total = lax.psum((weight_term, bias_term), "rows")
    grad_scale = 1.0 / math.sqrt(node_rows * lax.axis_size("rows"))
    grad_weight = weight_total * grad_scale
    grad_bias = bias_total * grad_scale
    partial_value = lax.dot_general(
        grad_pre, weight, (((1,), (1,)), ((), ())), preferred_element_type=jnp.float32
    )
    grad_agg = (
        lax.psum_scatter(partial_value, "cols", scatter_dimension=1, tiled=True)
        .astype(jnp.bfloat16)
        .reshape(clusters_here, tile_width, feat_half)
    )
    buckets = jnp.zeros(((levels + 1) * clusters_here, tile_width, feat_half), jnp.float32)
    buckets = sweep_slots(
        0,
        my_count,
        lambda carried, slot_ids, is_valid: spread_products(
            carried, adj_tiles, local_slots, tile_dst, slot_ids, is_valid, grad_agg, 0
        ),
        buckets,
    )
    summed = buckets[:clusters_here]
    for bit in range(levels):
        summed = summed + partner(
            buckets[(bit + 1) * clusters_here : (bit + 2) * clusters_here], "rows", bit
        )
    grad_features = (summed * live_node).reshape(node_rows, feat_half).astype(jnp.bfloat16)
    return (hidden, grad_weight, grad_bias, grad_features)


def solution(mesh):
    return jax.shard_map(
        local,
        mesh=mesh,
        in_specs=(
            P("rows", "cols"),
            P("rows", None, None),
            P("rows"),
            P("rows"),
            P("rows"),
            P("rows"),
            P(None, "cols"),
            P("cols"),
            P("rows", "cols"),
        ),
        out_specs=(P("rows", "cols"), P(None, "cols"), P("cols"), P("rows", "cols")),
        check_vma=False,
    )
```

profile of v0, /device:TPU:8, one launch (start us, length us, event | category | flops | bytes accessed | tf_op | source)
XLA Modules:
  0.0 193.4 jit_solution(5257428830742332566)
XLA Ops:
  8.7 1.3 fusion.10
  11.3 0.7 fusion.16
  12.0 0.8 reshape.169
  12.9 20.3 %all_gather.6 = bf16[32,128,64]{1,2,0:T(8,128)(2,1)S(1)} all-gather(bf16[2,128,64]{1,2,0:T(8,128)(2,1)S(1)} %copy.30), channel_id=1, replica_groups=mesh['rows'=16,'cols'=2] {'rows'}, dimensions={0}, use_global_device_ids=true | all-gather | bytes 557056 | tf_op jit(solution)/shard_map/all_gather | solution.py:84
  33.8 27.2 %while.20 = (s32[]{:T(128)}, f32[2,128,64]{1,2,0:T(8,128)S(1)}, s32[]{:T(128)}, s32[]{:T(128)}, s32[]{:T(128)}, /*index=5*/s32[96]{0:T(128)}, bf16[96,128,128]{2...) while((s32[]{:T(128)}, f32[2,128,64]{1,2,0:T(8,128)S(1)}, ...), condition=%wide.region_4.5_spmd, body=%wide.region_2.4_spmd.sunk | while | flops 33687796 | bytes 4465817 | solution.py:21
  34.5 1.3 gather_fusion
  35.8 0.7 fusion.47
  36.4 2.5 %gather_fusion.1 = bf16[16,128,128]{2,1,0:T(8,128)(2,1)S(1)} fusion(bf16[96,128,128]{2,1,0:T(8,128)(2,1)} %get-tuple-element.328, s32[1024]{0:T(1024)S(1)} %pad_clamp_fusion.8), kind=kCustom, calls=%fused_computation.1.clone.1 | custom fusion | bytes 1048640 | tf_op jit(solution)/shard_map/while/body/gather | solution.py:46
  39.0 1.3 gather_fusion.2
  41.5 1.4 scatter_fusion
  43.5 1.3 gather_fusion
  44.8 0.7 fusion.47
  45.5 2.5 %gather_fusion.1 = bf16[16,128,128]{2,1,0:T(8,128)(2,1)S(1)} fusion(bf16[96,128,128]{2,1,0:T(8,128)(2,1)} %get-tuple-element.328, s32[1024]{0:T(1024)S(1)} %pad_clamp_fusion.8), kind=kCustom, calls=%fused_computation.1.clone.1 | custom fusion | bytes 1048640 | tf_op jit(solution)/shard_map/while/body/gather | solution.py:46
  48.1 1.3 gather_fusion.2
  50.5 1.4 scatter_fusion
  52.6 1.3 gather_fusion
  53.9 0.7 fusion.47
  54.6 2.5 %gather_fusion.1 = bf16[16,128,128]{2,1,0:T(8,128)(2,1)S(1)} fusion(bf16[96,128,128]{2,1,0:T(8,128)(2,1)} %get-tuple-element.328, s32[1024]{0:T(1024)S(1)} %pad_clamp_fusion.8), kind=kCustom, calls=%fused_computation.1.clone.1 | custom fusion | bytes 1048640 | tf_op jit(solution)/shard_map/while/body/gather | solution.py:46
  57.1 1.3 gather_fusion.2
  59.6 1.4 scatter_fusion
  61.0 4.6 %all_gather.7 = bf16[256,128]{0,1:T(8,128)(2,1)S(1)} all-gather(bf16[256,64]{0,1:T(8,128)(2,1)S(1)} %copy_bitcast_fusion.1), channel_id=1, replica_groups=mesh['rows'=16,'cols'=2] {'cols'}, dimensions={1}, use_global_device_ids=true | all-gather | bytes 98304 | tf_op jit(solution)/shard_map/all_gather | solution.py:96
  65.6 0.9 convert_reduce_fusion
  66.5 0.8 fusion.21
  67.3 0.8 fusion.20
  68.2 48.7 %psum.15 = f32[128]{0:T(128)S(1)} all-reduce(f32[128]{0:T(128)S(1)} %get-tuple-element.184), channel_id=1, replica_groups=mesh['rows'=16,'cols'=2] {'rows'}, use_global_device_ids=true, to_apply=%region_7.8 | all-reduce | flops 128 | bytes 1024 | tf_op jit(solution)/shard_map/psum | solution.py:110
  117.4 0.8 convert_element_type.79
  118.4 22.8 %while.21 = (s32[]{:T(128)}, f32[10,128,64]{1,2,0:T(8,128)S(1)}, s32[]{:T(128)}, s32[]{:T(128)}, s32[96]{0:T(128)S(1)}, /*index=5*/bf16[96,128,128]{2,1,0:T(8,12...) while((s32[]{:T(128)}, f32[10,128,64]{1,2,0:T(8,128)S(1)}, s32[]{:T(128)}, ...), condition=%wide.region_11.12_spmd, body=%wide.region_9.11_spmd.sunk | while | flops 33687776 | bytes 4465797 | solution.py:21
  118.5 0.7 gather_fusion.4
  119.1 0.7 fusion.53
  119.8 2.5 %gather_fusion.5 = bf16[16,128,128]{2,1,0:T(8,128)(2,1)S(1)} fusion(bf16[96,128,128]{2,1,0:T(8,128)(2,1)} %get-tuple-element.358, s32[1024]{0:T(1024)S(1)} %pad_clamp_fusion.10), kind=kCustom, calls=%fused_computation.5.clone.1 | custom fusion | bytes 1048640 | tf_op jit(solution)/shard_map/while/body/gather | solution.py:59
  122.3 1.3 gather_fusion.6
  123.7 0.7 gather_fusion.7
  124.6 1.3 scatter_fusion.1
  126.0 0.7 gather_fusion.4
  126.7 0.7 fusion.53
  127.4 2.5 %gather_fusion.5 = bf16[16,128,128]{2,1,0:T(8,128)(2,1)S(1)} fusion(bf16[96,128,128]{2,1,0:T(8,128)(2,1)} %get-tuple-element.358, s32[1024]{0:T(1024)S(1)} %pad_clamp_fusion.10), kind=kCustom, calls=%fused_computation.5.clone.1 | custom fusion | bytes 1048640 | tf_op jit(solution)/shard_map/while/body/gather | solution.py:59
  129.9 1.3 gather_fusion.6
  131.3 0.7 gather_fusion.7
  132.2 1.4 scatter_fusion.1
  133.6 0.7 gather_fusion.4
  134.3 0.7 fusion.53
  134.9 2.6 %gather_fusion.5 = bf16[16,128,128]{2,1,0:T(8,128)(2,1)S(1)} fusion(bf16[96,128,128]{2,1,0:T(8,128)(2,1)} %get-tuple-element.358, s32[1024]{0:T(1024)S(1)} %pad_clamp_fusion.10), kind=kCustom, calls=%fused_computation.5.clone.1 | custom fusion | bytes 1048640 | tf_op jit(solution)/shard_map/while/body/gather | solution.py:59
  137.5 1.3 gather_fusion.6
  138.8 0.7 gather_fusion.7
  139.8 1.3 scatter_fusion.1
  141.6 23.7 %collective-permute-start.2 = (f32[2,128,64]{1,0,2:T(2,128)S(1)}, f32[2,128,64]{1,0,2:T(2,128)S(1)}, u32[]{:S(2)}, u32[]{:S(2)}) collective-permute-start(f32[2,128,64]{1,0,2:T(2,128)S(1)} %get-tuple-element.188), channel_id=1, source_target_pairs={{0,8},{2,10},{4,12},{6,14},{8,0},{10,2},{12,4},{14,6},{16,24},{18,... | collective-permute-start | bytes 196616 | tf_op jit(solution)/shard_map/ppermute | solution.py:11
  165.2 18.5 %all-reduce.2.cloned.1.call-done = f32[128,128]{1,0:T(8,128)} async-done(((f32[128,128]{1,0:T(8,128)}), f32[128,128]{1,0:T(8,128)}) %all-reduce.2.cloned.1.call-update) | async-done | bytes 65552 | tf_op jit(solution)/shard_map/psum | solution.py:110
  183.7 1.5 broadcast_multiply_fusion
  (63 shorter events, 6.9 us)
Async XLA Ops:
  8.0 57.6 %copy-start = (bf16[128,128]{1,0:T(8,128)(2,1)S(1)}, bf16[128,128]{1,0:T(8,128)(2,1)}, u32[]{:S(2)}) copy-start(bf16[128,128]{1,0:T(8,128)(2,1)} %param.19) | copy-start | bytes 98308
  8.0 109.4 %reduce-scatter.2.cloned.1.call-start = ((), (), s32[]{:S(2)}) async-start(), calls=%async_computation.2 | async-start | bytes 196608 | tf_op jit(solution)/shard_map/reduce_scatter | solution.py:118
  33.7 31.8 %copy-start.1 = (bf16[256,128]{1,0:T(8,128)(2,1)S(1)}, bf16[256,128]{1,0:T(8,128)(2,1)}, u32[]{:S(2)}) copy-start(bf16[256,128]{1,0:T(8,128)(2,1)} %param.21) | copy-start | bytes 196612
  33.7 31.8 %copy-start.2 = (f32[128]{0:T(128)S(1)}, f32[128]{0:T(128)}, u32[]{:S(2)}) copy-start(f32[128]{0:T(128)} %param.20) | copy-start | bytes 1540
  67.3 116.4 %all-reduce.2.cloned.1.call-start = ((), (), s32[]{:S(2)}) async-start(), calls=%async_computation.1 | async-start | bytes 131072 | tf_op jit(solution)/shard_map/psum | solution.py:110
  141.5 43.7 %collective-permute-start.3 = (f32[2,128,64]{1,0,2:T(2,128)S(1)}, f32[2,128,64]{1,0,2:T(2,128)S(1)}, u32[]{:S(2)}, u32[]{:S(2)}) collective-permute-start(f32[2,128,64]{1,0,2:T(2,128)S(1)} %get-tuple-element.187), channel_id=1, source_target_pairs={{0,16},{2,18},{4,20},{6,22},{8,24},{10,26},{12,28},{14,30},{16,0},... | collective-permute-start | bytes 196616 | tf_op jit(solution)/shard_map/ppermute | solution.py:11
  141.6 43.6 %collective-permute-start.2 = (f32[2,128,64]{1,0,2:T(2,128)S(1)}, f32[2,128,64]{1,0,2:T(2,128)S(1)}, u32[]{:S(2)}, u32[]{:S(2)}) collective-permute-start(f32[2,128,64]{1,0,2:T(2,128)S(1)} %get-tuple-element.188), channel_id=1, source_target_pairs={{0,8},{2,10},{4,12},{6,14},{8,0},{10,2},{12,4},{14,6},{16,24},{18,... | collective-permute-start | bytes 196616 | tf_op jit(solution)/shard_map/ppermute | solution.py:11
  165.2 20.0 %collective-permute-start.1 = (f32[2,128,64]{1,0,2:T(2,128)S(1)}, f32[2,128,64]{1,0,2:T(2,128)S(1)}, u32[]{:S(2)}, u32[]{:S(2)}) collective-permute-start(f32[2,128,64]{1,0,2:T(2,128)S(1)} %get-tuple-element.189), channel_id=1, source_target_pairs={{0,4},{2,6},{4,0},{6,2},{8,12},{10,14},{12,8},{14,10},{16,20},{18,... | collective-permute-start | bytes 196616 | tf_op jit(solution)/shard_map/ppermute | solution.py:11
  165.2 20.0 %collective-permute-start = (f32[2,128,64]{1,0,2:T(2,128)S(1)}, f32[2,128,64]{1,0,2:T(2,128)S(1)}, u32[]{:S(2)}, u32[]{:S(2)}) collective-permute-start(f32[2,128,64]{1,0,2:T(2,128)S(1)} %get-tuple-element.186), channel_id=1, source_target_pairs={{0,2},{2,0},{4,6},{6,4},{8,10},{10,8},{12,14},{14,12},{16,18},{18,... | collective-permute-start | bytes 196616 | tf_op jit(solution)/shard_map/ppermute | solution.py:11
Sparse Core Ops, SparseCore 0:
  67.4 33.8 reduce-scatter.1
Sparse Core Ops, SparseCore 1:
  71.8 111.9 all-reduce.1
where the time goes:
time: 195 us; the launch traced here: 193 us
  blocking collectives  73.6 us (38%)
  local copies, waits for them, and re-layouts  35.4 us (18%)
  starting transfers between devices  23.8 us (12%)
  waiting for transfers between devices  18.5 us (9%)
  between operations  17.6 us (9%)
  other arithmetic  17.2 us (9%)
  matrix products  4.85 us (2%)
  loops' own time  2.36 us (1%)
    psum x1, blocking collectives, local(): weight_total, bias_total = lax.psum((weight_term, bias_term), 'rows')  48.7 us
    ppermute x4, starting transfers between devices, partner(): lax.ppermute(shard, axis, [(i, i ^ 1 << distance) for i in range(lax.axis...  23.7 us
    all_gather x1, blocking collectives, local(): whole_rows = lax.all_gather(masked, 'rows', axis=0, tiled=True)  20.3 us
    psum x1, waiting for transfers between devices, local(): weight_total, bias_total = lax.psum((weight_term, bias_term), 'rows')  18.5 us
    gather x3, local copies, waits for them, and re-layouts, spread_products(): tile_block = tile_data[clamped]  7.64 us
    gather x3, local copies, waits for them, and re-layouts, gather_products(): tile_block = tile_data[clamped]  7.62 us
    all_gather x1, blocking collectives, local(): agg_full = lax.all_gather(agg_local, 'cols', axis=1, tiled=True)  4.58 us
    scatter-add x3, other arithmetic, gather_products(): return totals.at[placed].add(products, mode='drop')  4.07 us
  transfers between devices with their start and end apart: 6, of which 1 were waited for; matrix products, arithmetic and copies ran while one was open for 14% of the time, Pallas kernels for 0%

commit v1 on v0

--- a/solution.py
+++ b/solution.py
@@ -5,6 +5,16 @@
 from jax.sharding import PartitionSpec as P
 
 TILE_GROUP = 16
+
+
+def turned_line(shard, axis, dim):
+    size = lax.axis_size(axis)
+    block, tiles = (shard, [shard])
+    for _ in range(size - 1):
+        block = lax.ppermute(block, axis, [(i, (i + 1) % size) for i in range(size)])
+        tiles.insert(0, block)
+    line = jnp.concatenate(tiles, axis=dim)
+    return jnp.roll(line, (lax.axis_index(axis) + 1) * shard.shape[dim], axis=dim)
 
 
 def partner(shard, axis, distance):
@@ -81,7 +91,7 @@
     levels = lax.axis_size("rows").bit_length() - 1
     local_slots = neighbour_slots(tile_src, lax.axis_index("rows"), clusters_here, levels)
     zero_totals = jnp.zeros((clusters_here, tile_width, feat_half), jnp.float32)
-    whole_rows = lax.all_gather(masked, "rows", axis=0, tiled=True)
+    whole_rows = turned_line(masked, "rows", 0)
     row_count = whole_rows.shape[0]
     first_slot, last_slot = slot_bounds(tile_src, 0, my_count, 0, 0 + row_count)
     own_totals = sweep_slots(

time: 195 us -> 268 us (1.37)
  waiting for transfers between devices: 18.5 us -> 115 us
  blocking collectives: 73.6 us -> 53.5 us
  local copies, waits for them, and re-layouts: 35.4 us -> 31.8 us
    ppermute x0 -> x15, waiting for transfers between devices: none -> 69.3 us  [turned_line(): lax.ppermute(block, axis, [(i, (i + 1) % size) for i in range(size)])]
    all_gather x1 -> x0, blocking collectives: 20.3 us -> none  [local(): whole_rows = lax.all_gather(masked, 'rows', axis=0, tiled=True)]
    psum x1, waiting for transfers between devices: 18.5 us -> 36.4 us  [local(): weight_total, bias_total = lax.psum((weight_term, bias_term), 'rows')]
    reduce_scatter x1, waiting for transfers between devices: 0.01 us -> 9.32 us  [local(): lax.psum_scatter(partial_value, 'cols', scatter_dimension=1, tiled=True)]
  transfers between devices with their start and end apart: 6 -> 21, of which waited for: 1 -> 17; matrix products, arithmetic and copies ran while one was open for 14% -> 10% of each run, Pallas kernels for 0% -> 0%
where the time goes in v1:
time: 268 us; the launch traced here: 267 us
  waiting for transfers between devices  115 us (43%)
  blocking collectives  53.5 us (20%)
  local copies, waits for them, and re-layouts  31.8 us (12%)
  starting transfers between devices  24 us (9%)
  between operations  17.7 us (7%)
  other arithmetic  17.2 us (6%)
  matrix products  4.85 us (2%)
    ppermute x15, waiting for transfers between devices, turned_line(): lax.ppermute(block, axis, [(i, (i + 1) % size) for i in range(size)])  69.3 us
    psum x1, blocking collectives, local(): weight_total, bias_total = lax.psum((weight_term, bias_term), 'rows')  48.9 us
    psum x1, waiting for transfers between devices, local(): weight_total, bias_total = lax.psum((weight_term, bias_term), 'rows')  36.4 us
    ppermute x4, starting transfers between devices, partner(): lax.ppermute(shard, axis, [(i, i ^ 1 << distance) for i in range(lax.axis...  23.8 us
    reduce_scatter x1, waiting for transfers between devices, local(): lax.psum_scatter(partial_value, 'cols', scatter_dimension=1, tiled=True)  9.32 us
    gather x3, local copies, waits for them, and re-layouts, spread_products(): tile_block = tile_data[clamped]  7.66 us
    gather x3, local copies, waits for them, and re-layouts, gather_products(): tile_block = tile_data[clamped]  7.62 us
  transfers between devices with their start and end apart: 21, of which 17 were waited for; matrix products, arithmetic and copies ran while one was open for 10% of the time, Pallas kernels for 0%

profile of v1, /device:TPU:8, one launch (start us, length us, event | category | flops | bytes accessed | tf_op | source)
XLA Modules:
  0.0 266.5 jit_solution(16894380970347908411)
XLA Ops:
  8.1 0.7 fusion.16
  8.8 0.8 reshape.169
  9.7 4.2 %collective-permute-done = bf16[2,128,64]{1,0,2:T(2,128)(2,1)S(1)} collective-permute-done((bf16[2,128,64]{1,0,2:T(2,128)(2,1)S(1)}, bf16[2,128,64]{1,0,2:T(2,128)(2,1)S(1)}, u32[]{:S(2)}, u32[]{:S(2)}) %collective-permute-start) | collective-permute-done | bytes 32800 | tf_op jit(solution)/shard_map/ppermute | solution.py:14
  13.9 4.2 %collective-permute-done.1 = bf16[2,128,64]{1,0,2:T(2,128)(2,1)S(1)} collective-permute-done((bf16[2,128,64]{1,0,2:T(2,128)(2,1)S(1)}, bf16[2,128,64]{1,0,2:T(2,128)(2,1)S(1)}, u32[]{:S(2)}, u32[]{:S(2)}) %collective-permute-start.1) | collective-permute-done | bytes 32800 | tf_op jit(solution)/shard_map/ppermute | solution.py:14
  18.2 4.2 %collective-permute-done.2 = bf16[2,128,64]{1,0,2:T(2,128)(2,1)S(1)} collective-permute-done((bf16[2,128,64]{1,0,2:T(2,128)(2,1)S(1)}, bf16[2,128,64]{1,0,2:T(2,128)(2,1)S(1)}, u32[]{:S(2)}, u32[]{:S(2)}) %collective-permute-start.2) | collective-permute-done | bytes 32800 | tf_op jit(solution)/shard_map/ppermute | solution.py:14
  22.4 4.2 %collective-permute-done.3 = bf16[2,128,64]{1,0,2:T(2,128)(2,1)S(1)} collective-permute-done((bf16[2,128,64]{1,0,2:T(2,128)(2,1)S(1)}, bf16[2,128,64]{1,0,2:T(2,128)(2,1)S(1)}, u32[]{:S(2)}, u32[]{:S(2)}) %collective-permute-start.3) | collective-permute-done | bytes 32800 | tf_op jit(solution)/shard_map/ppermute | solution.py:14
  26.6 4.2 %collective-permute-done.4 = bf16[2,128,64]{1,0,2:T(2,128)(2,1)S(1)} collective-permute-done((bf16[2,128,64]{1,0,2:T(2,128)(2,1)S(1)}, bf16[2,128,64]{1,0,2:T(2,128)(2,1)S(1)}, u32[]{:S(2)}, u32[]{:S(2)}) %collective-permute-start.4) | collective-permute-done | bytes 32800 | tf_op jit(solution)/shard_map/ppermute | solution.py:14
  30.9 4.2 %collective-permute-done.5 = bf16[2,128,64]{1,0,2:T(2,128)(2,1)S(1)} collective-permute-done((bf16[2,128,64]{1,0,2:T(2,128)(2,1)S(1)}, bf16[2,128,64]{1,0,2:T(2,128)(2,1)S(1)}, u32[]{:S(2)}, u32[]{:S(2)}) %collective-permute-start.5) | collective-permute-done | bytes 32800 | tf_op jit(solution)/shard_map/ppermute | solution.py:14
  35.1 4.2 %collective-permute-done.6 = bf16[2,128,64]{1,0,2:T(2,128)(2,1)S(1)} collective-permute-done((bf16[2,128,64]{1,0,2:T(2,128)(2,1)S(1)}, bf16[2,128,64]{1,0,2:T(2,128)(2,1)S(1)}, u32[]{:S(2)}, u32[]{:S(2)}) %collective-permute-start.6) | collective-permute-done | bytes 32800 | tf_op jit(solution)/shard_map/ppermute | solution.py:14
  39.4 4.2 %collective-permute-done.7 = bf16[2,128,64]{1,0,2:T(2,128)(2,1)S(1)} collective-permute-done((bf16[2,128,64]{1,0,2:T(2,128)(2,1)S(1)}, bf16[2,128,64]{1,0,2:T(2,128)(2,1)S(1)}, u32[]{:S(2)}, u32[]{:S(2)}) %collective-permute-start.7) | collective-permute-done | bytes 32800 | tf_op jit(solution)/shard_map/ppermute | solution.py:14
  43.6 4.2 %collective-permute-done.8 = bf16[2,128,64]{1,0,2:T(2,128)(2,1)S(1)} collective-permute-done((bf16[2,128,64]{1,0,2:T(2,128)(2,1)S(1)}, bf16[2,128,64]{1,0,2:T(2,128)(2,1)S(1)}, u32[]{:S(2)}, u32[]{:S(2)}) %collective-permute-start.8) | collective-permute-done | bytes 32800 | tf_op jit(solution)/shard_map/ppermute | solution.py:14
  47.8 4.4 %collective-permute-done.9 = bf16[2,128,64]{1,0,2:T(2,128)(2,1)S(1)} collective-permute-done((bf16[2,128,64]{1,0,2:T(2,128)(2,1)S(1)}, bf16[2,128,64]{1,0,2:T(2,128)(2,1)S(1)}, u32[]{:S(2)}, u32[]{:S(2)}) %collective-permute-start.9) | collective-permute-done | bytes 32800 | tf_op jit(solution)/shard_map/ppermute | solution.py:14
  52.2 6.0 %collective-permute-done.10 = bf16[2,128,64]{1,0,2:T(2,128)(2,1)S(1)} collective-permute-done((bf16[2,128,64]{1,0,2:T(2,128)(2,1)S(1)}, bf16[2,128,64]{1,0,2:T(2,128)(2,1)S(1)}, u32[]{:S(2)}, u32[]{:S(2)}) %collective-permute-start.10) | collective-permute-done | bytes 32800 | tf_op jit(solution)/shard_map/ppermute | solution.py:14
  58.3 6.0 %collective-permute-done.11 = bf16[2,128,64]{1,0,2:T(2,128)(2,1)S(1)} collective-permute-done((bf16[2,128,64]{1,0,2:T(2,128)(2,1)S(1)}, bf16[2,128,64]{1,0,2:T(2,128)(2,1)S(1)}, u32[]{:S(2)}, u32[]{:S(2)}) %collective-permute-start.11) | collective-permute-done | bytes 32800 | tf_op jit(solution)/shard_map/ppermute | solution.py:14
  64.3 6.0 %collective-permute-done.12 = bf16[2,128,64]{1,0,2:T(2,128)(2,1)S(1)} collective-permute-done((bf16[2,128,64]{1,0,2:T(2,128)(2,1)S(1)}, bf16[2,128,64]{1,0,2:T(2,128)(2,1)S(1)}, u32[]{:S(2)}, u32[]{:S(2)}) %collective-permute-start.12) | collective-permute-done | bytes 32800 | tf_op jit(solution)/shard_map/ppermute | solution.py:14
  71.0 5.4 %collective-permute-done.13 = bf16[2,128,64]{1,0,2:T(2,128)(2,1)S(1)} collective-permute-done((bf16[2,128,64]{1,0,2:T(2,128)(2,1)S(1)}, bf16[2,128,64]{1,0,2:T(2,128)(2,1)S(1)}, u32[]{:S(2)}, u32[]{:S(2)}) %collective-permute-start.13) | collective-permute-done | bytes 32800 | tf_op jit(solution)/shard_map/ppermute | solution.py:14
  76.4 1.3 fusion.10
  79.0 3.4 %collective-permute-done.14 = bf16[2,128,64]{1,0,2:T(2,128)(2,1)S(1)} collective-permute-done((bf16[2,128,64]{1,0,2:T(2,128)(2,1)S(1)}, bf16[2,128,64]{1,0,2:T(2,128)(2,1)S(1)}, u32[]{:S(2)}, u32[]{:S(2)}) %collective-permute-start.14) | collective-permute-done | bytes 32800 | tf_op jit(solution)/shard_map/ppermute | solution.py:14
  82.4 1.9 concatenate.6
  84.5 0.7 copy.20
  85.3 23.2 %while.20 = (s32[]{:T(128)}, f32[2,128,64]{1,2,0:T(8,128)S(1)}, s32[]{:T(128)}, s32[]{:T(128)}, s32[]{:T(128)}, /*index=5*/s32[96]{0:T(128)S(1)}, bf16[96,128,12...) while((s32[]{:T(128)}, f32[2,128,64]{1,2,0:T(8,128)S(1)}, ...), condition=%wide.region_4.5_spmd, body=%wide.region_2.4_spmd.sunk | while | flops 33687796 | bytes 4465817 | solution.py:31
  87.3 2.5 gather_fusion.1
  91.7 1.4 scatter_fusion
  95.0 2.5 gather_fusion.1
  99.4 1.4 scatter_fusion
  102.8 2.5 gather_fusion.1
  107.1 1.4 scatter_fusion
  108.5 4.6 %all_gather.3 = bf16[256,128]{0,1:T(8,128)(2,1)S(1)} all-gather(bf16[256,64]{0,1:T(8,128)(2,1)S(1)} %copy_bitcast_fusion.1), channel_id=1, replica_groups=mesh['rows'=16,'cols'=2] {'cols'}, dimensions={1}, use_global_device_ids=true | all-gather | bytes 98304 | tf_op jit(solution)/shard_map/all_gather | solution.py:106
  113.1 0.9 convert_reduce_fusion
  114.0 48.9 %psum.15 = f32[128]{0:T(128)S(1)} all-reduce(f32[128]{0:T(128)S(1)} %get-tuple-element.167), channel_id=1, replica_groups=mesh['rows'=16,'cols'=2] {'rows'}, use_global_device_ids=true, to_apply=%region_7.8 | all-reduce | flops 128 | bytes 1024 | tf_op jit(solution)/shard_map/psum | solution.py:120
  163.0 0.8 fusion.21
  164.4 0.8 fusion.20
  165.2 9.3 %reduce-scatter.2.cloned.1.call-done = f32[256,64]{0,1:T(8,128)} async-done(((f32[256,128]{0,1:T(8,128)}), f32[256,64]{0,1:T(8,128)}) %reduce-scatter.2.cloned.1.call-update) | async-done | bytes 65552 | tf_op jit(solution)/shard_map/reduce_scatter | solution.py:128
  174.5 0.8 convert_element_type.79
  175.5 20.8 %while.21 = (s32[]{:T(128)}, f32[10,128,64]{1,2,0:T(8,128)S(1)}, s32[]{:T(128)}, s32[]{:T(128)}, s32[96]{0:T(128)S(1)}, /*index=5*/bf16[96,128,128]{2,1,0:T(8,12...) while((s32[]{:T(128)}, f32[10,128,64]{1,2,0:T(8,128)S(1)}, s32[]{:T(128)}, ...), condition=%wide.region_11.12_spmd, body=%wide.region_9.11_spmd.sunk | while | flops 33687776 | bytes 4465797 | solution.py:31
  176.2 0.7 fusion.53
  176.9 2.6 gather_fusion.5
  181.1 1.3 scatter_fusion.1
  183.1 0.7 fusion.53
  183.8 2.6 gather_fusion.5
  188.0 1.4 scatter_fusion.1
  190.1 0.7 fusion.53
  190.7 2.6 gather_fusion.5
  194.9 1.3 scatter_fusion.1
  196.6 2.5 collective-permute-start.18
  199.1 21.3 %collective-permute-start.17 = (f32[2,128,64]{1,0,2:T(2,128)S(1)}, f32[2,128,64]{1,0,2:T(2,128)S(1)}, u32[]{:S(2)}, u32[]{:S(2)}) collective-permute-start(f32[2,128,64]{1,0,2:T(2,128)S(1)} %get-tuple-element.171), channel_id=1, source_target_pairs={{0,8},{2,10},{4,12},{6,14},{8,0},{10,2},{12,4},{14,6},{16,24},{18,... | collective-permute-start | bytes 196616 | tf_op jit(solution)/shard_map/ppermute | solution.py:21
  220.4 36.4 %all-reduce.2.cloned.1.call-done = f32[128,128]{1,0:T(8,128)} async-done(((f32[128,128]{1,0:T(8,128)}), f32[128,128]{1,0:T(8,128)}) %all-reduce.2.cloned.1.call-update) | async-done | bytes 65552 | tf_op jit(solution)/shard_map/psum | solution.py:120
  256.9 1.5 broadcast_multiply_fusion
  (97 shorter events, 18.5 us)
Async XLA Ops:
  8.0 105.1 %copy-start = (bf16[128,128]{1,0:T(8,128)(2,1)S(1)}, bf16[128,128]{1,0:T(8,128)(2,1)}, u32[]{:S(2)}) copy-start(bf16[128,128]{1,0:T(8,128)(2,1)} %param.19) | copy-start | bytes 98308
  8.0 77.2 %copy-start.2 = (s32[96]{0:T(128)S(1)}, s32[96]{0:T(128)}, u32[]{:S(2)}) copy-start(s32[96]{0:T(128)} %param.15) | copy-start | bytes 1156
  8.0 77.2 %copy-start.1 = (s32[96]{0:T(128)S(1)}, s32[96]{0:T(128)}, u32[]{:S(2)}) copy-start(s32[96]{0:T(128)} %param.16) | copy-start | bytes 1156
  8.0 166.4 %reduce-scatter.2.cloned.1.call-start = ((), (), s32[]{:S(2)}) async-start(), calls=%async_computation.2 | async-start | bytes 196608 | tf_op jit(solution)/shard_map/reduce_scatter | solution.py:128
  9.6 4.3 %collective-permute-start = (bf16[2,128,64]{1,0,2:T(2,128)(2,1)S(1)}, bf16[2,128,64]{1,0,2:T(2,128)(2,1)S(1)}, u32[]{:S(2)}, u32[]{:S(2)}) collective-permute-start(bf16[2,128,64]{1,0,2:T(2,128)(2,1)S(1)} %multiply_convert_fusion.3), channel_id=1, source_target_pairs={{0,2},{2,4},{4,6},{6,8},{8,10},{10,12},{12,14},{14,16},{16,18},{18... | collective-permute-start | bytes 98312 | tf_op jit(solution)/shard_map/ppermute | solution.py:14
  13.9 4.2 %collective-permute-start.1 = (bf16[2,128,64]{1,0,2:T(2,128)(2,1)S(1)}, bf16[2,128,64]{1,0,2:T(2,128)(2,1)S(1)}, u32[]{:S(2)}, u32[]{:S(2)}) collective-permute-start(bf16[2,128,64]{1,0,2:T(2,128)(2,1)S(1)} %collective-permute-done), channel_id=1, source_target_pairs={{0,2},{2,4},{4,6},{6,8},{8,10},{10,12},{12,14},{14,16},{16,18},{18... | collective-permute-start | bytes 98312 | tf_op jit(solution)/shard_map/ppermute | solution.py:14
  18.2 4.2 %collective-permute-start.2 = (bf16[2,128,64]{1,0,2:T(2,128)(2,1)S(1)}, bf16[2,128,64]{1,0,2:T(2,128)(2,1)S(1)}, u32[]{:S(2)}, u32[]{:S(2)}) collective-permute-start(bf16[2,128,64]{1,0,2:T(2,128)(2,1)S(1)} %collective-permute-done.1), channel_id=1, source_target_pairs={{0,2},{2,4},{4,6},{6,8},{8,10},{10,12},{12,14},{14,16},{16,18},{18... | collective-permute-start | bytes 98312 | tf_op jit(solution)/shard_map/ppermute | solution.py:14
  22.4 4.2 %collective-permute-start.3 = (bf16[2,128,64]{1,0,2:T(2,128)(2,1)S(1)}, bf16[2,128,64]{1,0,2:T(2,128)(2,1)S(1)}, u32[]{:S(2)}, u32[]{:S(2)}) collective-permute-start(bf16[2,128,64]{1,0,2:T(2,128)(2,1)S(1)} %collective-permute-done.2), channel_id=1, source_target_pairs={{0,2},{2,4},{4,6},{6,8},{8,10},{10,12},{12,14},{14,16},{16,18},{18... | collective-permute-start | bytes 98312 | tf_op jit(solution)/shard_map/ppermute | solution.py:14
  26.6 4.2 %collective-permute-start.4 = (bf16[2,128,64]{1,0,2:T(2,128)(2,1)S(1)}, bf16[2,128,64]{1,0,2:T(2,128)(2,1)S(1)}, u32[]{:S(2)}, u32[]{:S(2)}) collective-permute-start(bf16[2,128,64]{1,0,2:T(2,128)(2,1)S(1)} %collective-permute-done.3), channel_id=1, source_target_pairs={{0,2},{2,4},{4,6},{6,8},{8,10},{10,12},{12,14},{14,16},{16,18},{18... | collective-permute-start | bytes 98312 | tf_op jit(solution)/shard_map/ppermute | solution.py:14
  30.9 4.2 %collective-permute-start.5 = (bf16[2,128,64]{1,0,2:T(2,128)(2,1)S(1)}, bf16[2,128,64]{1,0,2:T(2,128)(2,1)S(1)}, u32[]{:S(2)}, u32[]{:S(2)}) collective-permute-start(bf16[2,128,64]{1,0,2:T(2,128)(2,1)S(1)} %collective-permute-done.4), channel_id=1, source_target_pairs={{0,2},{2,4},{4,6},{6,8},{8,10},{10,12},{12,14},{14,16},{16,18},{18... | collective-permute-start | bytes 98312 | tf_op jit(solution)/shard_map/ppermute | solution.py:14
  35.1 4.2 %collective-permute-start.6 = (bf16[2,128,64]{1,0,2:T(2,128)(2,1)S(1)}, bf16[2,128,64]{1,0,2:T(2,128)(2,1)S(1)}, u32[]{:S(2)}, u32[]{:S(2)}) collective-permute-start(bf16[2,128,64]{1,0,2:T(2,128)(2,1)S(1)} %collective-permute-done.5), channel_id=1, source_target_pairs={{0,2},{2,4},{4,6},{6,8},{8,10},{10,12},{12,14},{14,16},{16,18},{18... | collective-permute-start | bytes 98312 | tf_op jit(solution)/shard_map/ppermute | solution.py:14
  39.4 4.2 %collective-permute-start.7 = (bf16[2,128,64]{1,0,2:T(2,128)(2,1)S(1)}, bf16[2,128,64]{1,0,2:T(2,128)(2,1)S(1)}, u32[]{:S(2)}, u32[]{:S(2)}) collective-permute-start(bf16[2,128,64]{1,0,2:T(2,128)(2,1)S(1)} %collective-permute-done.6), channel_id=1, source_target_pairs={{0,2},{2,4},{4,6},{6,8},{8,10},{10,12},{12,14},{14,16},{16,18},{18... | collective-permute-start | bytes 98312 | tf_op jit(solution)/shard_map/ppermute | solution.py:14
  43.6 4.2 %collective-permute-start.8 = (bf16[2,128,64]{1,0,2:T(2,128)(2,1)S(1)}, bf16[2,128,64]{1,0,2:T(2,128)(2,1)S(1)}, u32[]{:S(2)}, u32[]{:S(2)}) collective-permute-start(bf16[2,128,64]{1,0,2:T(2,128)(2,1)S(1)} %collective-permute-done.7), channel_id=1, source_target_pairs={{0,2},{2,4},{4,6},{6,8},{8,10},{10,12},{12,14},{14,16},{16,18},{18... | collective-permute-start | bytes 98312 | tf_op jit(solution)/shard_map/ppermute | solution.py:14
  47.8 4.4 %collective-permute-start.9 = (bf16[2,128,64]{1,0,2:T(2,128)(2,1)S(1)}, bf16[2,128,64]{1,0,2:T(2,128)(2,1)S(1)}, u32[]{:S(2)}, u32[]{:S(2)}) collective-permute-start(bf16[2,128,64]{1,0,2:T(2,128)(2,1)S(1)} %collective-permute-done.8), channel_id=1, source_target_pairs={{0,2},{2,4},{4,6},{6,8},{8,10},{10,12},{12,14},{14,16},{16,18},{18... | collective-permute-start | bytes 98312 | tf_op jit(solution)/shard_map/ppermute | solution.py:14
  52.2 6.0 %collective-permute-start.10 = (bf16[2,128,64]{1,0,2:T(2,128)(2,1)S(1)}, bf16[2,128,64]{1,0,2:T(2,128)(2,1)S(1)}, u32[]{:S(2)}, u32[]{:S(2)}) collective-permute-start(bf16[2,128,64]{1,0,2:T(2,128)(2,1)S(1)} %collective-permute-done.9), channel_id=1, source_target_pairs={{0,2},{2,4},{4,6},{6,8},{8,10},{10,12},{12,14},{14,16},{16,18},{18... | collective-permute-start | bytes 98312 | tf_op jit(solution)/shard_map/ppermute | solution.py:14
  58.3 6.0 %collective-permute-start.11 = (bf16[2,128,64]{1,0,2:T(2,128)(2,1)S(1)}, bf16[2,128,64]{1,0,2:T(2,128)(2,1)S(1)}, u32[]{:S(2)}, u32[]{:S(2)}) collective-permute-start(bf16[2,128,64]{1,0,2:T(2,128)(2,1)S(1)} %collective-permute-done.10), channel_id=1, source_target_pairs={{0,2},{2,4},{4,6},{6,8},{8,10},{10,12},{12,14},{14,16},{16,18},{18... | collective-permute-start | bytes 98312 | tf_op jit(solution)/shard_map/ppermute | solution.py:14
  64.3 6.0 %collective-permute-start.12 = (bf16[2,128,64]{1,0,2:T(2,128)(2,1)S(1)}, bf16[2,128,64]{1,0,2:T(2,128)(2,1)S(1)}, u32[]{:S(2)}, u32[]{:S(2)}) collective-permute-start(bf16[2,128,64]{1,0,2:T(2,128)(2,1)S(1)} %collective-permute-done.11), channel_id=1, source_target_pairs={{0,2},{2,4},{4,6},{6,8},{8,10},{10,12},{12,14},{14,16},{16,18},{18... | collective-permute-start | bytes 98312 | tf_op jit(solution)/shard_map/ppermute | solution.py:14
  70.3 6.0 %collective-permute-start.13 = (bf16[2,128,64]{1,0,2:T(2,128)(2,1)S(1)}, bf16[2,128,64]{1,0,2:T(2,128)(2,1)S(1)}, u32[]{:S(2)}, u32[]{:S(2)}) collective-permute-start(bf16[2,128,64]{1,0,2:T(2,128)(2,1)S(1)} %collective-permute-done.12), channel_id=1, source_target_pairs={{0,2},{2,4},{4,6},{6,8},{8,10},{10,12},{12,14},{14,16},{16,18},{18... | collective-permute-start | bytes 98312 | tf_op jit(solution)/shard_map/ppermute | solution.py:14
  76.4 6.0 %collective-permute-start.14 = (bf16[2,128,64]{1,0,2:T(2,128)(2,1)S(1)}, bf16[2,128,64]{1,0,2:T(2,128)(2,1)S(1)}, u32[]{:S(2)}, u32[]{:S(2)}) collective-permute-start(bf16[2,128,64]{1,0,2:T(2,128)(2,1)S(1)} %collective-permute-done.13), channel_id=1, source_target_pairs={{0,2},{2,4},{4,6},{6,8},{8,10},{10,12},{12,14},{14,16},{16,18},{18... | collective-permute-start | bytes 98312 | tf_op jit(solution)/shard_map/ppermute | solution.py:14
  85.3 27.9 %copy-start.3 = (bf16[256,128]{1,0:T(8,128)(2,1)S(1)}, bf16[256,128]{1,0:T(8,128)(2,1)}, u32[]{:S(2)}) copy-start(bf16[256,128]{1,0:T(8,128)(2,1)} %param.21) | copy-start | bytes 196612
  85.3 27.8 %copy-start.4 = (f32[128]{0:T(128)S(1)}, f32[128]{0:T(128)}, u32[]{:S(2)}) copy-start(f32[128]{0:T(128)} %param.20) | copy-start | bytes 1540
  163.8 93.1 %all-reduce.2.cloned.1.call-start = ((), (), s32[]{:S(2)}) async-start(), calls=%async_computation.1 | async-start | bytes 131072 | tf_op jit(solution)/shard_map/psum | solution.py:120
  196.6 61.7 %collective-permute-start.18 = (f32[2,128,64]{1,0,2:T(2,128)S(1)}, f32[2,128,64]{1,0,2:T(2,128)S(1)}, u32[]{:S(2)}, u32[]{:S(2)}) collective-permute-start(f32[2,128,64]{1,0,2:T(2,128)S(1)} %get-tuple-element.170), channel_id=1, source_target_pairs={{0,16},{2,18},{4,20},{6,22},{8,24},{10,26},{12,28},{14,30},{16,0},... | collective-permute-start | bytes 196616 | tf_op jit(solution)/shard_map/ppermute | solution.py:21
  199.1 59.3 %collective-permute-start.17 = (f32[2,128,64]{1,0,2:T(2,128)S(1)}, f32[2,128,64]{1,0,2:T(2,128)S(1)}, u32[]{:S(2)}, u32[]{:S(2)}) collective-permute-start(f32[2,128,64]{1,0,2:T(2,128)S(1)} %get-tuple-element.171), channel_id=1, source_target_pairs={{0,8},{2,10},{4,12},{6,14},{8,0},{10,2},{12,4},{14,6},{16,24},{18,... | collective-permute-start | bytes 196616 | tf_op jit(solution)/shard_map/ppermute | solution.py:21
  220.4 37.9 %collective-permute-start.16 = (f32[2,128,64]{1,0,2:T(2,128)S(1)}, f32[2,128,64]{1,0,2:T(2,128)S(1)}, u32[]{:S(2)}, u32[]{:S(2)}) collective-permute-start(f32[2,128,64]{1,0,2:T(2,128)S(1)} %get-tuple-element.172), channel_id=1, source_target_pairs={{0,4},{2,6},{4,0},{6,2},{8,12},{10,14},{12,8},{14,10},{16,20},{18,... | collective-permute-start | bytes 196616 | tf_op jit(solution)/shard_map/ppermute | solution.py:21
  220.4 37.9 %collective-permute-start.15 = (f32[2,128,64]{1,0,2:T(2,128)S(1)}, f32[2,128,64]{1,0,2:T(2,128)S(1)}, u32[]{:S(2)}, u32[]{:S(2)}) collective-permute-start(f32[2,128,64]{1,0,2:T(2,128)S(1)} %get-tuple-element.169), channel_id=1, source_target_pairs={{0,2},{2,0},{4,6},{6,4},{8,10},{10,8},{12,14},{14,12},{16,18},{18,... | collective-permute-start | bytes 196616 | tf_op jit(solution)/shard_map/ppermute | solution.py:21
Sparse Core Ops, SparseCore 0:
  163.9 10.5 reduce-scatter.1
Sparse Core Ops, SparseCore 1:
  168.3 88.5 all-reduce.1
